TPU v7x, 32 devices: a whole 2x2x4 slice. The times are simulated.
32 devices in a mesh: seq: 16 (over z, y, core), dp: 2 (over x).
Axes of the slice: x: 2, y: 2, z: 4, core: 2. Of those that a mesh axis runs over, the one named last changes fastest.
Arguments:
- layer_input: bfloat16 [2, 2048, 4096], P('dp', 'seq'), may hold values from -0.3125 to 0.3125
- scan_input: bfloat16 [2, 2048, 2048], P('dp', 'seq'), may hold values from -6 to 6
- readout: bfloat16 [2, 2048, 64], P('dp', 'seq'), may hold values from -6 to 6
- log_decay: float32 [2, 2048, 32], P('dp', 'seq'), may hold values from -1 to 0
- output_cotangent: bfloat16 [2, 2048, 2048], P('dp', 'seq'), may hold values from -0.0078125 to 0.0078125
- write_weight: float32 [4096, 64], P('dp'), may hold values from -6 to 6
- first_moment: float32 [4096, 64], P('dp'), may hold values from -6 to 6
- second_moment: float32 [4096, 64], P('dp'), may hold values from 1 to 25
Outputs:
- decay_gradient: float32 [2, 2048, 32], P('dp', 'seq')
- new_weight: float32 [4096, 64], P('dp')
- new_first: float32 [4096, 64], P('dp')
- new_second: float32 [4096, 64], P('dp')
All inputs are finite; a program needn't handle non-finite values.
Results may differ from a plain program's by a relative error of at most 0.0039.
Values may be sent and summed in bfloat16 or wider, within the bound.
A program may use at most 64 MiB of HBM per device.

v0:
```python
import jax
import jax.numpy as jnp
from jax import lax
from jax.sharding import PartitionSpec as P

HALF_HEAD_COUNT = 32
HEAD_DIM = 64
STATE = 64
beta_one = 0.9
beta_two = 0.999
adam_count = 10.0
learn_rate = 0.01
weight_decay = 0.1
epsilon = 1e-08
highest = lax.Precision.HIGHEST


def entering(part, axis, combine, identity, reverse):
    count = lax.axis_size(axis)
    place = lax.axis_index(axis)
    ahead = count - 1 - place if reverse else place
    gathered = jax.tree.map(lambda a: lax.all_gather(a, axis), part)
    state = jax.tree.map(lambda a, e: jnp.zeros_like(a) + jnp.asarray(e, a.dtype), part, identity)

    def one(lap, state):
        source = count - 1 - lap if reverse else lap
        return combine(
            state, jax.tree.map(lambda a: lax.dynamic_index_in_dim(a, source, 0, False), gathered)
        )

    return lax.fori_loop(0, ahead, one, state)


def pair_combine(earlier_pair, later_pair):
    return (
        earlier_pair[0] * later_pair[0],
        later_pair[0][:, None, None] * earlier_pair[1] + later_pair[1],
    )


def adam_update(grad_rows, weight_rows, first_rows, second_rows):
    new_first = beta_one * first_rows + (1.0 - beta_one) * grad_rows
    new_second = beta_two * second_rows + (1.0 - beta_two) * grad_rows * grad_rows
    first_hat = new_first / (1.0 - beta_one**adam_count)
    second_hat = new_second / (1.0 - beta_two**adam_count)
    new_weight = weight_rows - learn_rate * (
        first_hat / (jnp.sqrt(second_hat) + epsilon) + weight_decay * weight_rows
    )
    return (new_weight, new_first, new_second)


def on_device(
    layer_input,
    scan_input,
    readout,
    log_decay,
    output_cotangent,
    write_weight,
    first_moment,
    second_moment,
):
    input_rows = layer_input[0]
    scan_rows = scan_input[0]
    read_rows = readout[0]
    decay_rows = log_decay[0]
    back_rows = output_cotangent[0]
    length = input_rows.shape[0]
    weight_half = write_weight.astype(jnp.bfloat16)
    write_sum = jnp.dot(
        input_rows,
        lax.all_gather(weight_half, "dp", axis=0, tiled=True),
        preferred_element_type=jnp.float32,
    )
    write_half = write_sum.astype(jnp.bfloat16)
    write_float = lax.optimization_barrier(write_half).astype(jnp.float32)
    running = jnp.cumsum(decay_rows, axis=0)
    overall = running[-1]
    to_end = jnp.exp(overall[None, :] - running)
    from_start = jnp.exp(running)
    scan_split = scan_rows.reshape(length, HALF_HEAD_COUNT, HEAD_DIM)
    back_split = back_rows.reshape(length, HALF_HEAD_COUNT, HEAD_DIM)
    scan_heads = scan_split.astype(jnp.float32)
    back_heads = back_split.astype(jnp.float32)
    read_float = read_rows.astype(jnp.float32)
    state_local = jnp.einsum(
        "shp,sn->hpn", scan_heads * to_end[:, :, None], write_float, precision=highest
    )
    reverse_local = jnp.einsum(
        "shp,sn->hpn", back_heads * from_start[:, :, None], read_float, precision=highest
    )
    decay_total = jnp.exp(overall)
    identity = (
        jnp.ones((HALF_HEAD_COUNT,), jnp.float32),
        jnp.zeros((HALF_HEAD_COUNT, HEAD_DIM, STATE), jnp.float32),
    )
    state_pair = entering((decay_total, state_local), "seq", pair_combine, identity, False)
    grad_pair = entering((decay_total, reverse_local), "seq", pair_combine, identity, True)
    state_before = state_pair[1]
    grad_after = grad_pair[1]
    term_one = decay_total * jnp.sum(grad_after * state_before, axis=(1, 2))
    grad_write = jnp.einsum("hpn,sn->shp", grad_after, write_float, precision=highest)
    second_rows = to_end * jnp.sum(scan_heads * grad_write, axis=2)
    term_two = jnp.cumsum(second_rows, axis=0) - second_rows
    state_read = jnp.einsum("hpn,sn->shp", state_before, read_float, precision=highest)
    third_rows = from_start * jnp.sum(back_heads * state_read, axis=2)
    term_three = jnp.flip(jnp.cumsum(jnp.flip(third_rows, 0), axis=0), 0)
    crossed = jnp.einsum("thp,shp->hts", scan_split, back_split, preferred_element_type=jnp.float32)
    heads_running = running.T
    spread = heads_running[:, None, :] - heads_running[:, :, None]
    row_index = lax.broadcasted_iota(jnp.int32, (length, length), 0)
    col_index = lax.broadcasted_iota(jnp.int32, (length, length), 1)
    kernel_mat = (
        jnp.where((row_index <= col_index)[None], jnp.exp(jnp.minimum(spread, 0.0)), 0.0) * crossed
    )
    write_read = jnp.dot(write_half, read_rows.T, preferred_element_type=jnp.float32)
    pairing = jnp.where((row_index < col_index)[None], kernel_mat * write_read[None], 0.0)
    balance = (jnp.sum(pairing, axis=2) - jnp.sum(pairing, axis=1)).T
    term_four = jnp.cumsum(balance, axis=0) - balance
    decay_grad = term_one[None, :] + term_two + term_three + term_four
    scaled_scan = (scan_heads * to_end[:, :, None]).reshape(length, HALF_HEAD_COUNT * HEAD_DIM)
    write_grad = jnp.dot(
        scaled_scan, grad_after.reshape(HALF_HEAD_COUNT * HEAD_DIM, STATE), precision=highest
    )
    write_grad = write_grad + jnp.dot(jnp.sum(kernel_mat, axis=0), read_float, precision=highest)
    grad_half = write_grad.astype(jnp.bfloat16)
    partial_grad = jnp.dot(input_rows.T, grad_half, preferred_element_type=jnp.float32)
    owner_grad = lax.psum_scatter(partial_grad, "dp", scatter_dimension=0, tiled=True)
    grad_rows = lax.psum(owner_grad, "seq")
    new_weight, new_first, new_second = adam_update(
        grad_rows, write_weight, first_moment, second_moment
    )
    return (decay_grad[None], new_weight, new_first, new_second)


def solution(mesh):
    in_specs = (
        P("dp", "seq", None),
        P("dp", "seq", None),
        P("dp", "seq", None),
        P("dp", "seq", None),
        P("dp", "seq", None),
        P("dp", None),
        P("dp", None),
        P("dp", None),
    )
    out_specs = (P("dp", "seq", None), P("dp", None), P("dp", None), P("dp", None))
    return jax.shard_map(
        on_device, mesh=mesh, in_specs=in_specs, out_specs=out_specs, check_vma=False
    )
```

profile of v0, /device:TPU:29, one launch (start us, length us, event | category | flops | bytes accessed | tf_op | source)
XLA Modules:
  0.0 436.1 jit_solution(12412782208266294412)
XLA Ops:
  7.2 0.9 copy.43
  8.4 1.3 copy.44
  9.8 1.6 fusion.17
  11.9 7.8 %all_gather.24 = bf16[4096,64]{0,1:T(8,128)(2,1)S(1)} all-gather(bf16[2048,64]{0,1:T(8,128)(2,1)S(1)} %convert_element_type.22), channel_id=1, replica_groups=mesh['seq'=16,'dp'=2] {'dp'}, dimensions={0}, use_global_device_ids=true | all-gather | bytes 786432 | tf_op jit(solution)/shard_map/all_gather | solution.py:71
  20.3 18.4 %all-gather.2 = f32[16,1,32]{2,1,0:T(1,128)S(1)} all-gather(f32[1,1,32]{2,1,0:T(1,128)S(1)} %get-tuple-element.175), channel_id=1, replica_groups=mesh['seq'=16,'dp'=2] {'seq'}, dimensions={0}, use_global_device_ids=true | all-gather | bytes 2176 | tf_op jit(solution)/shard_map/all_gather | solution.py:22
  38.9 1.8 fusion
  40.8 95.8 %all-gather.6.cloned.1.call-done = f32[512,64,64]{2,1,0:T(8,128)} async-done(((f32[32,64,64]{2,1,0:T(8,128)}), f32[512,64,64]{2,1,0:T(8,128)}) %all-gather.6.cloned.1.call-update) | async-done | bytes 8388624 | tf_op jit(solution)/shard_map/all_gather | solution.py:22
  137.4 1.9 fusion.7
  139.5 1.3 convolution_bitcast_fusion
  140.9 42.5 %reduce-scatter.2.cloned.1.call-done = f32[2048,64]{0,1:T(8,128)} async-done(((f32[4096,64]{0,1:T(8,128)}), f32[2048,64]{0,1:T(8,128)}) %reduce-scatter.2.cloned.1.call-update) | async-done | bytes 524304 | tf_op jit(solution)/shard_map/reduce_scatter | solution.py:127
  183.4 1.6 fusion.4
  185.8 90.6 %all-reduce.2.cloned.1.call-done = f32[2048,64]{0,1:T(8,128)} async-done(((f32[2048,64]{0,1:T(8,128)}), f32[2048,64]{0,1:T(8,128)}) %all-reduce.2.cloned.1.call-update) | async-done | bytes 524304 | tf_op jit(solution)/shard_map/psum | solution.py:128
  276.4 2.7 multiply_subtract_fusion
  279.2 125.0 %all-gather.8.cloned.1.call-done = f32[512,64,64]{2,1,0:T(8,128)} async-done(((f32[32,64,64]{2,1,0:T(8,128)}), f32[512,64,64]{2,1,0:T(8,128)}) %all-gather.8.cloned.1.call-update) | async-done | bytes 8388624 | tf_op jit(solution)/shard_map/all_gather | solution.py:22
  404.3 22.4 %while.27 = (s32[]{:T(128)}, f32[32,64,64]{2,1,0:T(8,128)S(1)}, s32[]{:T(128)}, f32[16,32]{1,0:T(8,128)S(1)}, f32[16,32,64,64]{3,2,1,0:T(8,128)}, /*index=5*/s32[]{:T(128)}, s32[]{:T(128)}, s32[]{:T(128)}) while((s32[]{:T(128)}, f32[32,64,64]{2,1,0:T(8,128)S(1)}, s32[]{:T(128)}, f32[16,32]{1,0:T(8,128)S(1)}, f32[16,32,64,64]{3,2,1,0:T(8,128)}, ...), condition=%wide.region_4.5_spmd, body=%wide.region_3.4_spmd.sunk | while | flops 262149 | bytes 1573375 | solution.py:31
  404.3 1.4 bitcast_add_fusion.5
  405.8 1.4 bitcast_add_fusion.5
  407.3 1.4 bitcast_add_fusion.5
  408.8 1.4 bitcast_add_fusion.5
  410.3 1.4 bitcast_add_fusion.5
  411.8 1.4 bitcast_add_fusion.5
  413.3 1.4 bitcast_add_fusion.5
  414.8 1.4 bitcast_add_fusion.5
  416.3 1.4 bitcast_add_fusion.5
  417.8 1.4 bitcast_add_fusion.5
  419.3 1.4 bitcast_add_fusion.5
  420.8 1.4 bitcast_add_fusion.5
  422.3 1.4 bitcast_add_fusion.5
  423.8 1.4 bitcast_add_fusion.5
  425.3 1.4 bitcast_add_fusion.5
  427.1 0.7 copy-done.2
  428.9 0.7 add_bitcast_fusion
  (68 shorter events, 5.1 us)
Async XLA Ops:
  7.2 12.6 %copy-start = (bf16[1,128,4096]{2,1,0:T(8,128)(2,1)S(1)}, bf16[1,128,4096]{2,1,0:T(8,128)(2,1)}, u32[]{:S(2)}) copy-start(bf16[1,128,4096]{2,1,0:T(8,128)(2,1)} %param.12) | copy-start | bytes 3145732
  7.2 2.6 copy-start.5
  7.2 129.4 %all-gather.6.cloned.1.call-start = ((), (), s32[]{:S(2)}) async-start(), calls=%async_computation.3 | async-start | bytes 17825792 | tf_op jit(solution)/shard_map/all_gather | solution.py:22
  9.7 29.2 %copy-start.1 = (bf16[1,128,2048]{1,2,0:T(8,128)(2,1)}, bf16[1,128,2048]{1,2,0:T(8,128)(2,1)S(1)}, u32[]{:S(2)}) copy-start(bf16[1,128,2048]{1,2,0:T(8,128)(2,1)S(1)} %copy.44) | copy-start | bytes 1572868
  9.7 1.9 copy-start.4
  9.8 2.0 copy-start.3
  11.5 171.9 %reduce-scatter.2.cloned.1.call-start = ((), (), s32[]{:S(2)}) async-start(), calls=%async_computation.1 | async-start | bytes 1572864 | tf_op jit(solution)/shard_map/reduce_scatter | solution.py:127
  140.8 135.6 %all-reduce.2.cloned.1.call-start = ((), (), s32[]{:S(2)}) async-start(), calls=%async_computation.2 | async-start | bytes 1048576 | tf_op jit(solution)/shard_map/psum | solution.py:128
  183.4 220.8 %all-gather.8.cloned.1.call-start = ((), (), s32[]{:S(2)}) async-start(), calls=%async_computation.4 | async-start | bytes 17825792 | tf_op jit(solution)/shard_map/all_gather | solution.py:22
  426.8 1.0 copy-start.2
Sparse Core Ops, SparseCore 0:
  11.6 124.9 all-gather.5
  140.9 42.3 reduce-scatter.1
  186.8 89.6 all-reduce.1
  278.4 125.7 all-gather.7
where the time goes:
time: 437 us; the launch traced here: 436 us
  waiting for transfers between devices  354 us (81%)
  other arithmetic  26.4 us (6%)
  blocking collectives  26.2 us (6%)
  between operations  14 us (3%)
  matrix products  10.4 us (2%)
    all_gather x2, waiting for transfers between devices, entering(): gathered = jax.tree.map(lambda a: lax.all_gather(a, axis), part)  221 us
    psum x1, waiting for transfers between devices, on_device(): grad_rows = lax.psum(owner_grad, 'seq')  90.6 us
    reduce_scatter x1, waiting for transfers between devices, on_device(): lax.psum_scatter(partial_grad, 'dp', scatter_dimension=0, tiled=True)  42.5 us
    add x15, other arithmetic, pair_combine(): later_pair[0][:, None, None] * earlier_pair[1] + later_pair[1]  21.7 us
    all_gather x1, blocking collectives, entering(): gathered = jax.tree.map(lambda a: lax.all_gather(a, axis), part)  18.4 us
  transfers between devices with their start and end apart: 4, of which 4 were waited for; matrix products, arithmetic and copies ran while one was open for 2% of the time, Pallas kernels for 0%

commit v1 on v0

--- a/solution.py
+++ b/solution.py
@@ -125,7 +125,8 @@
     grad_half = write_grad.astype(jnp.bfloat16)
     partial_grad = jnp.dot(input_rows.T, grad_half, preferred_element_type=jnp.float32)
     owner_grad = lax.psum_scatter(partial_grad, "dp", scatter_dimension=0, tiled=True)
-    grad_rows = lax.psum(owner_grad, "seq")
+    x_now = lax.all_gather(owner_grad, "seq")
+    grad_rows = jnp.sum(x_now, 0)
     new_weight, new_first, new_second = adam_update(
         grad_rows, write_weight, first_moment, second_moment
     )

time: 437 us -> 407 us (0.931)
  waiting for transfers between devices: 354 us -> 311 us
  local copies, waits for them, and re-layouts: 4.35 us -> 11.8 us
    psum x1 -> x0, waiting for transfers between devices: 90.6 us -> none  [on_device(): grad_rows = lax.psum(owner_grad, 'seq')]
    all_gather x0 -> x1, waiting for transfers between devices: none -> 49 us  [on_device(): x_now = lax.all_gather(owner_grad, 'seq')]
    unnamed x14 -> x19, local copies, waits for them, and re-layouts: 2.36 us -> 9.79 us
  transfers between devices with their start and end apart: 4 -> 4, of which waited for: 4 -> 4; matrix products, arithmetic and copies ran while one was open for 2% -> 8% of each run, Pallas kernels for 0% -> 0%
where the time goes in v1:
time: 407 us; the launch traced here: 403 us
  waiting for transfers between devices  311 us (76%)
  other arithmetic  26.9 us (7%)
  blocking collectives  26.2 us (6%)
  between operations  14.1 us (3%)
  local copies, waits for them, and re-layouts  11.8 us (3%)
  matrix products  11.5 us (3%)
    all_gather x2, waiting for transfers between devices, entering(): gathered = jax.tree.map(lambda a: lax.all_gather(a, axis), part)  221 us
    all_gather x1, waiting for transfers between devices, on_device(): x_now = lax.all_gather(owner_grad, 'seq')  49 us
    reduce_scatter x1, waiting for transfers between devices, on_device(): lax.psum_scatter(partial_grad, 'dp', scatter_dimension=0, tiled=True)  40.7 us
    add x15, other arithmetic, pair_combine(): later_pair[0][:, None, None] * earlier_pair[1] + later_pair[1]  21.8 us
    all_gather x1, blocking collectives, entering(): gathered = jax.tree.map(lambda a: lax.all_gather(a, axis), part)  18.4 us
    unnamed x19, local copies, waits for them, and re-layouts  9.79 us
  transfers between devices with their start and end apart: 4, of which 4 were waited for; matrix products, arithmetic and copies ran while one was open for 8% of the time, Pallas kernels for 0%

profile of v1, /device:TPU:29, one launch (start us, length us, event | category | flops | bytes accessed | tf_op | source)
XLA Modules:
  0.0 402.6 jit_solution(10034673811869322434)
XLA Ops:
  8.4 1.3 copy.44
  9.8 1.6 fusion.17
  11.9 7.8 %all_gather.30 = bf16[4096,64]{0,1:T(8,128)(2,1)S(1)} all-gather(bf16[2048,64]{0,1:T(8,128)(2,1)S(1)} %convert_element_type.22), channel_id=1, replica_groups=mesh['seq'=16,'dp'=2] {'dp'}, dimensions={0}, use_global_device_ids=true | all-gather | bytes 786432 | tf_op jit(solution)/shard_map/all_gather | solution.py:71
  20.3 18.4 %all-gather.3 = f32[16,1,32]{2,1,0:T(1,128)S(1)} all-gather(f32[1,1,32]{2,1,0:T(1,128)S(1)} %get-tuple-element.175), channel_id=1, replica_groups=mesh['seq'=16,'dp'=2] {'seq'}, dimensions={0}, use_global_device_ids=true | all-gather | bytes 2176 | tf_op jit(solution)/shard_map/all_gather | solution.py:22
  38.9 1.8 fusion
  40.8 95.8 %all-gather.8.cloned.1.call-done = f32[512,64,64]{2,1,0:T(8,128)} async-done(((f32[32,64,64]{2,1,0:T(8,128)}), f32[512,64,64]{2,1,0:T(8,128)}) %all-gather.8.cloned.1.call-update) | async-done | bytes 8388624 | tf_op jit(solution)/shard_map/all_gather | solution.py:22
  137.4 1.9 fusion.7
  139.5 1.3 convolution_bitcast_fusion
  140.9 1.7 fusion.4
  142.7 40.7 %reduce-scatter.2.cloned.1.call-done = f32[2048,64]{0,1:T(8,128)} async-done(((f32[4096,64]{0,1:T(8,128)}), f32[2048,64]{0,1:T(8,128)}) %reduce-scatter.2.cloned.1.call-update) | async-done | bytes 524304 | tf_op jit(solution)/shard_map/reduce_scatter | solution.py:127
  184.1 125.6 %all-gather.10.cloned.1.call-done = f32[512,64,64]{2,1,0:T(8,128)} async-done(((f32[32,64,64]{2,1,0:T(8,128)}), f32[512,64,64]{2,1,0:T(8,128)}) %all-gather.10.cloned.1.call-update) | async-done | bytes 8388624 | tf_op jit(solution)/shard_map/all_gather | solution.py:22
  309.8 22.8 %while.27 = (s32[]{:T(128)}, f32[32,64,64]{2,1,0:T(8,128)S(1)}, s32[]{:T(128)}, f32[16,32]{1,0:T(8,128)S(1)}, f32[16,32,64,64]{3,2,1,0:T(8,128)}, /*index=5*/s32[]{:T(128)}, s32[]{:T(128)}, s32[]{:T(128)}) while((s32[]{:T(128)}, f32[32,64,64]{2,1,0:T(8,128)S(1)}, s32[]{:T(128)}, f32[16,32]{1,0:T(8,128)S(1)}, f32[16,32,64,64]{3,2,1,0:T(8,128)}, ...), condition=%wide.region_4.5_spmd, body=%wide.region_3.4_spmd.sunk | while | flops 262149 | bytes 1573375 | solution.py:31
  309.9 1.4 bitcast_add_fusion.5
  311.4 1.4 bitcast_add_fusion.5
  312.9 1.4 bitcast_add_fusion.5
  314.3 1.4 bitcast_add_fusion.5
  315.8 1.4 bitcast_add_fusion.5
  317.3 1.4 bitcast_add_fusion.5
  318.8 1.5 bitcast_add_fusion.5
  320.3 1.5 bitcast_add_fusion.5
  321.9 1.5 bitcast_add_fusion.5
  323.4 1.4 bitcast_add_fusion.5
  324.9 1.5 bitcast_add_fusion.5
  326.4 1.4 bitcast_add_fusion.5
  327.9 1.5 bitcast_add_fusion.5
  329.4 1.4 bitcast_add_fusion.5
  330.9 1.4 bitcast_add_fusion.5
  332.6 1.7 fusion.6
  335.8 49.0 %all-gather.12.cloned.1.call-done = f32[32768,64]{0,1:T(8,128)} async-done(((f32[2048,64]{0,1:T(8,128)}), f32[32768,64]{0,1:T(8,128)}) %all-gather.12.cloned.1.call-update) | async-done | bytes 8388624 | tf_op jit(solution)/shard_map/all_gather | solution.py:128
  384.8 8.1 %copy.59 = f32[8,8,16,2048]{3,2,1,0:T(8,128)S(1)} copy(f32[8,8,16,2048]{3,1,2,0:T(8,128)} %bitcast.89) | data formatting | bytes 16777216
  393.0 1.7 bitcast_reduce_fusion
  394.7 1.4 multiply_subtract_fusion
  (74 shorter events, 6.1 us)
Async XLA Ops:
  7.2 12.6 %copy-start = (bf16[1,128,4096]{2,1,0:T(8,128)(2,1)S(1)}, bf16[1,128,4096]{2,1,0:T(8,128)(2,1)}, u32[]{:S(2)}) copy-start(bf16[1,128,4096]{2,1,0:T(8,128)(2,1)} %param.12) | copy-start | bytes 3145732
  7.2 2.6 copy-start.7
  7.2 129.4 %all-gather.8.cloned.1.call-start = ((), (), s32[]{:S(2)}) async-start(), calls=%async_computation.2 | async-start | bytes 17825792 | tf_op jit(solution)/shard_map/all_gather | solution.py:22
  9.7 29.2 %copy-start.1 = (bf16[1,128,2048]{1,2,0:T(8,128)(2,1)}, bf16[1,128,2048]{1,2,0:T(8,128)(2,1)S(1)}, u32[]{:S(2)}) copy-start(bf16[1,128,2048]{1,2,0:T(8,128)(2,1)S(1)} %copy.44) | copy-start | bytes 1572868
  9.7 1.9 copy-start.6
  9.8 2.0 copy-start.2
  11.5 171.9 %reduce-scatter.2.cloned.1.call-start = ((), (), s32[]{:S(2)}) async-start(), calls=%async_computation.1 | async-start | bytes 1572864 | tf_op jit(solution)/shard_map/reduce_scatter | solution.py:127
  140.8 168.9 %all-gather.10.cloned.1.call-start = ((), (), s32[]{:S(2)}) async-start(), calls=%async_computation.3 | async-start | bytes 17825792 | tf_op jit(solution)/shard_map/all_gather | solution.py:22
  142.6 242.2 %all-gather.12.cloned.1.call-start = ((), (), s32[]{:S(2)}) async-start(), calls=%async_computation.4 | async-start | bytes 8912896 | tf_op jit(solution)/shard_map/all_gather | solution.py:128
  392.9 1.8 copy-start.3
  392.9 1.8 copy-start.4
  392.9 1.8 copy-start.5
Sparse Core Ops, SparseCore 0:
  11.6 124.9 all-gather.7
  141.0 42.3 reduce-scatter.1
  185.5 124.1 all-gather.9
  311.7 73.0 all-gather.11
